TPU v7x, 256 devices: a whole 4x4x8 slice. The times are simulated.
256 devices in a mesh: floor: 8 (over x, core), facade: 32 (over z, y).
Axes of the slice: x: 4, y: 4, z: 8, core: 2. Of those that a mesh axis runs over, the one named last changes fastest.
Arguments:
- interface_rhs: float32 [8, 32, 2, 256, 128], P('floor', 'facade'), may hold values from -40 to 40
- inverse_factor: float32 [8, 32, 1024, 1024], P('floor', 'facade')
- near_coupling: bfloat16 [8, 32, 1024, 1024], P('floor', 'facade'), may hold values from -0.09375 to 0.09375
- near_pattern: int32 [8, 32, 8, 8], P('floor', 'facade'), may hold values from 0 to 1, as said below
Outputs:
- multipliers: float32 [8, 32, 2, 256, 128], P('floor', 'facade')
- residual: float32 [8, 32, 2, 256, 128], P('floor', 'facade')
Inputs may be any that keep to these rules, and one draw needn't show every extreme that they name: `near_pattern`: every diagonal block is set; each subdomain has from 8 to 32 blocks set, and in every draw some subdomain has exactly 32.
All inputs are finite; a program needn't handle non-finite values.
Results may differ from a plain program's by a relative error of at most 0.0022.
Values sent between devices are 32-bit elements; how exact they have to be, the bound alone decides.
A program may use at most 64 MiB of HBM per device.

v0:
```python
import jax
import jax.numpy as jnp
from jax import lax
from jax.sharding import PartitionSpec as P

ITERS = 4


finest = lax.Precision.HIGHEST


def shifted(value, axis, steps):
    count = lax.axis_size(axis)
    first, last = (max(0, -steps), min(count, count - steps))
    return lax.ppermute(value, axis, [(source, source + steps) for source in range(first, last)])


def from_behind(value, axis, steps):
    count = lax.axis_size(axis)
    pairs = [(source, (source + steps) % count) for source in range(count)]
    return lax.ppermute(value, axis, pairs)


def owned_inner(left_side, right_side):
    return jnp.sum(left_side * right_side, axis=(0, 1))


def local(interface_rhs, inverse_factor, near_coupling, near_pattern):
    factor = inverse_factor[0, 0]
    coupling = near_coupling[0, 0]
    pattern = near_pattern[0, 0]
    faces = interface_rhs.shape[3]
    cases = interface_rhs.shape[4]
    width_all = 4 * faces
    blocks = pattern.shape[0]
    block_rows = width_all // blocks
    floor_pos = lax.axis_index("floor")
    floors = lax.axis_size("floor")
    top_keep = (floor_pos < floors - 1).astype(jnp.float32)
    expanded = jnp.repeat(jnp.repeat(pattern, block_rows, axis=0), block_rows, axis=1).astype(
        jnp.bfloat16
    )
    masked = coupling * expanded
    rhs_owned = jnp.stack([interface_rhs[0, 0, 0] * top_keep, interface_rhs[0, 0, 1]])
    multipliers = jnp.zeros_like(rhs_owned)
    residual = rhs_owned

    def norm_of(vector):
        return lax.psum(owned_inner(vector, vector), ("floor", "facade"))

    direction = rhs_owned
    norm_now = norm_of(residual)
    for sweep in range(ITERS):
        below = shifted(direction[0], "floor", 1)
        beside = from_behind(direction[1], "facade", 1)
        apply_flat = jnp.stack([-below, direction[0], -beside, direction[1]]).reshape(
            width_all, cases
        )
        inner = jnp.dot(factor, apply_flat, precision=finest, preferred_element_type=jnp.float32)
        outer = jnp.einsum(
            "ji,jr->ir", factor, inner, precision=finest, preferred_element_type=jnp.float32
        )
        rounded = apply_flat.astype(jnp.bfloat16)
        forward = jnp.dot(masked, rounded, preferred_element_type=jnp.float32).astype(jnp.bfloat16)
        image = (
            outer + jnp.einsum("ji,jr->ir", masked, forward, preferred_element_type=jnp.float32)
        ).reshape(4, faces, cases)
        above = shifted(image[0], "floor", -1)
        beyond = from_behind(image[2], "facade", -1)
        image = jnp.stack([(image[1] - above) * top_keep, image[3] - beyond])
        step_size = norm_now / lax.psum(owned_inner(direction, image), ("floor", "facade"))
        multipliers = multipliers + step_size * direction
        residual = residual - step_size * image
        if sweep + 1 < ITERS:
            norm_next = norm_of(residual)
            direction = residual + norm_next / norm_now * direction
            norm_now = norm_next
    return (multipliers[None, None], residual[None, None])


def solution(mesh):
    placed = (
        P("floor", "facade", None, None, None),
        P("floor", "facade", None, None),
        P("floor", "facade", None, None),
        P("floor", "facade", None, None),
    )
    return jax.shard_map(
        local,
        mesh=mesh,
        in_specs=placed,
        out_specs=(P("floor", "facade", None, None, None), P("floor", "facade", None, None, None)),
        check_vma=False,
    )
```

profile of v0, /device:TPU:1, one launch (start us, length us, event | category | flops | bytes accessed | tf_op | source)
XLA Modules:
  0.0 693.5 jit_solution(7314364137194731607)
XLA Ops:
  1.8 4.5 collective-permute-start
  8.5 2.9 broadcast_in_dim.5
  15.1 3.4 mul.272
  21.3 6.7 fusion.14
  28.0 3.0 fusion.70
  31.1 4.6 fusion.27
  37.6 4.4 collective-permute-done.2
  42.7 7.2 %collective-permute-start.3 = (f32[256,128]{0,1:T(8,128)S(1)}, f32[256,128]{0,1:T(8,128)S(1)}, u32[]{:S(2)}, u32[]{:S(2)}) collective-permute-start(f32[256,128]{0,1:T(8,128)S(1)} %get-tuple-element.40), channel_id=1, source_target_pairs={{0,31},{1,0},{2,1},{3,2},{4,3},{5,4},{6,5},{7,6},{8,7},{9,8},{10,9... | collective-permute-start | bytes 393224 | tf_op jit(solution)/shard_map/ppermute | solution.py:21
  52.6 77.5 %all-reduce = (f32[128]{0:T(128)S(1)}, f32[128]{0:T(128)S(1)}) all-reduce(f32[128]{0:T(128)S(1)} %get-tuple-element.7, f32[128]{0:T(128)S(1)} %get-tuple-element.6), channel_id=1, replica_groups=mesh['floor'=8,'facade'=32] {'floor','facade'}, use_global_device_ids=true, to_apply=%region_1.0 | all-reduce | flops 256 | bytes 2048 | tf_op jit(solution)/shard_map/psum | solution.py:49
  130.3 73.4 %psum.58 = f32[128]{0:T(128)S(1)} all-reduce(f32[128]{0:T(128)S(1)} %multiply_reduce_fusion.4), channel_id=1, replica_groups=mesh['floor'=8,'facade'=32] {'floor','facade'}, use_global_device_ids=true, to_apply=%region_5.0 | all-reduce | flops 128 | bytes 1024 | tf_op jit(solution)/shard_map/psum | solution.py:49
  207.1 4.5 collective-permute-done.5
  213.7 7.5 %fusion.10 = f32[128,1024]{1,0:T(8,128)} fusion(f32[1024,128]{1,0:T(8,128)S(1)} %bitcast.183, f32[1,1,1024,1024]{3,2,1,0:T(8,128)} %param.5), kind=kOutput, calls=%fused_computation.10 | convolution fusion | flops 1610612736 | bytes 5242880 | tf_op jit(solution)/shard_map/dot_general | solution.py:59
  222.0 3.9 fusion.67
  225.9 4.7 fusion.33
  230.7 3.5 collective-permute-start.6
  240.4 78.1 %psum.59 = f32[128]{0:T(128)S(1)} all-reduce(f32[128]{0:T(128)S(1)} %multiply_reduce_fusion.3), channel_id=1, replica_groups=mesh['floor'=8,'facade'=32] {'floor','facade'}, use_global_device_ids=true, to_apply=%region_7.0 | all-reduce | flops 128 | bytes 1024 | tf_op jit(solution)/shard_map/psum | solution.py:71
  318.8 72.4 %psum.60 = f32[128]{0:T(128)S(1)} all-reduce(f32[128]{0:T(128)S(1)} %get-tuple-element.10), channel_id=1, replica_groups=mesh['floor'=8,'facade'=32] {'floor','facade'}, use_global_device_ids=true, to_apply=%region_9.0 | all-reduce | flops 128 | bytes 1024 | tf_op jit(solution)/shard_map/psum | solution.py:49
  391.7 2.5 collective-permute-start.8
  394.3 4.8 collective-permute-done.9
  402.1 7.6 %fusion.6 = f32[128,1024]{1,0:T(8,128)} fusion(f32[1024,128]{1,0:T(8,128)} %bitcast.184, f32[1,1,1024,1024]{3,2,1,0:T(8,128)} %param.5), kind=kOutput, calls=%fused_computation.6 | convolution fusion | flops 1610612736 | bytes 5242880 | tf_op jit(solution)/shard_map/dot_general | solution.py:59
  409.9 3.8 fusion.64
  413.7 4.9 fusion.39
  418.6 3.4 collective-permute-start.10
  428.2 77.6 %psum.61 = f32[128]{0:T(128)S(1)} all-reduce(f32[128]{0:T(128)S(1)} %multiply_reduce_fusion.1), channel_id=1, replica_groups=mesh['floor'=8,'facade'=32] {'floor','facade'}, use_global_device_ids=true, to_apply=%region_11.0 | all-reduce | flops 128 | bytes 1024 | tf_op jit(solution)/shard_map/psum | solution.py:71
  506.1 72.6 %psum.62 = f32[128]{0:T(128)S(1)} all-reduce(f32[128]{0:T(128)S(1)} %multiply_reduce_fusion), channel_id=1, replica_groups=mesh['floor'=8,'facade'=32] {'floor','facade'}, use_global_device_ids=true, to_apply=%region_13.0 | all-reduce | flops 128 | bytes 1024 | tf_op jit(solution)/shard_map/psum | solution.py:49
  579.8 2.5 collective-permute-start.12
  582.3 4.8 collective-permute-done.13
  588.2 6.7 fusion.2
  596.7 3.0 fusion.61
  599.7 4.6 fusion.45
  604.5 3.6 collective-permute-start.14
  613.5 77.6 %psum.63 = f32[128]{0:T(128)S(1)} all-reduce(f32[128]{0:T(128)S(1)} %fusion.74), channel_id=1, replica_groups=mesh['floor'=8,'facade'=32] {'floor','facade'}, use_global_device_ids=true, to_apply=%region_15.0 | all-reduce | flops 128 | bytes 1024 | tf_op jit(solution)/shard_map/psum | solution.py:71
  (124 shorter events, 49.7 us)
Async XLA Ops:
  1.7 18.4 %copy-start.3 = (f32[1,1,1,256,128]{3,4,2,1,0:T(8,128)}, f32[1,1,1,256,128]{3,4,2,1,0:T(8,128)S(1)}, u32[]{:S(2)}) copy-start(f32[1,1,1,256,128]{3,4,2,1,0:T(8,128)S(1)} %copy.34) | copy-start | bytes 393220
  1.8 18.4 %collective-permute-start = (f32[256,128]{0,1:T(8,128)S(1)}, f32[256,128]{0,1:T(8,128)S(1)}, u32[]{:S(2)}, u32[]{:S(2)}) collective-permute-start(f32[256,128]{0,1:T(8,128)S(1)} %fusion.121), channel_id=1, source_target_pairs={{0,32},{32,64},{64,96},{96,128},{128,160},{160,192},{192,224},{1,3... | collective-permute-start | bytes 393224 | tf_op jit(solution)/shard_map/ppermute | solution.py:15
  6.4 13.8 %collective-permute-start.1 = (f32[256,128]{0,1:T(8,128)S(1)}, f32[256,128]{0,1:T(8,128)S(1)}, u32[]{:S(2)}, u32[]{:S(2)}) collective-permute-start(f32[256,128]{0,1:T(8,128)S(1)} %bitcast.173), channel_id=1, source_target_pairs={{0,1},{1,2},{2,3},{3,4},{4,5},{5,6},{6,7},{7,8},{8,9},{9,10},{10,1... | collective-permute-start | bytes 393224 | tf_op jit(solution)/shard_map/ppermute | solution.py:21
  15.0 3.4 copy-start.1
  15.0 3.5 copy-start.2
  35.7 6.3 collective-permute-start.2
  42.7 9.1 %collective-permute-start.3 = (f32[256,128]{0,1:T(8,128)S(1)}, f32[256,128]{0,1:T(8,128)S(1)}, u32[]{:S(2)}, u32[]{:S(2)}) collective-permute-start(f32[256,128]{0,1:T(8,128)S(1)} %get-tuple-element.40), channel_id=1, source_target_pairs={{0,31},{1,0},{2,1},{3,2},{4,3},{5,4},{6,5},{7,6},{8,7},{9,8},{10,9... | collective-permute-start | bytes 393224 | tf_op jit(solution)/shard_map/ppermute | solution.py:21
  203.8 7.8 %collective-permute-start.5 = (f32[256,128]{0,1:T(8,128)S(1)}, f32[256,128]{0,1:T(8,128)S(1)}, u32[]{:S(2)}, u32[]{:S(2)}) collective-permute-start(f32[256,128]{0,1:T(8,128)S(1)} %get-tuple-element.50), channel_id=1, source_target_pairs={{0,1},{1,2},{2,3},{3,4},{4,5},{5,6},{6,7},{7,8},{8,9},{9,10},{10,1... | collective-permute-start | bytes 393224 | tf_op jit(solution)/shard_map/ppermute | solution.py:21
  204.5 7.1 %collective-permute-start.4 = (f32[256,128]{0,1:T(8,128)S(1)}, f32[256,128]{0,1:T(8,128)S(1)}, u32[]{:S(2)}, u32[]{:S(2)}) collective-permute-start(f32[256,128]{0,1:T(8,128)S(1)} %get-tuple-element.49), channel_id=1, source_target_pairs={{0,32},{32,64},{64,96},{96,128},{128,160},{160,192},{192,224},{1,3... | collective-permute-start | bytes 393224 | tf_op jit(solution)/shard_map/ppermute | solution.py:15
  222.0 3.9 copy-start.5
  230.7 7.0 %collective-permute-start.6 = (f32[256,128]{0,1:T(8,128)S(1)}, f32[256,128]{0,1:T(8,128)S(1)}, u32[]{:S(2)}, u32[]{:S(2)}) collective-permute-start(f32[256,128]{0,1:T(8,128)S(1)} %get-tuple-element.38), channel_id=1, source_target_pairs={{32,0},{64,32},{96,64},{128,96},{160,128},{192,160},{224,192},{33,... | collective-permute-start | bytes 393224 | tf_op jit(solution)/shard_map/ppermute | solution.py:15
  234.2 5.3 collective-permute-start.7
  391.1 8.9 %copy-start.14 = (f32[128]{0:T(128)}, f32[128]{0:T(128)S(1)}, u32[]{:S(2)}) copy-start(f32[128]{0:T(128)S(1)} %div.24) | copy-start | bytes 1540
  391.3 7.8 %collective-permute-start.9 = (f32[256,128]{0,1:T(8,128)S(1)}, f32[256,128]{0,1:T(8,128)S(1)}, u32[]{:S(2)}, u32[]{:S(2)}) collective-permute-start(f32[256,128]{0,1:T(8,128)S(1)} %get-tuple-element.46), channel_id=1, source_target_pairs={{0,1},{1,2},{2,3},{3,4},{4,5},{5,6},{6,7},{7,8},{8,9},{9,10},{10,1... | collective-permute-start | bytes 393224 | tf_op jit(solution)/shard_map/ppermute | solution.py:21
  391.7 7.4 %collective-permute-start.8 = (f32[256,128]{0,1:T(8,128)S(1)}, f32[256,128]{0,1:T(8,128)S(1)}, u32[]{:S(2)}, u32[]{:S(2)}) collective-permute-start(f32[256,128]{0,1:T(8,128)S(1)} %get-tuple-element.45), channel_id=1, source_target_pairs={{0,32},{32,64},{64,96},{96,128},{128,160},{160,192},{192,224},{1,3... | collective-permute-start | bytes 393224 | tf_op jit(solution)/shard_map/ppermute | solution.py:15
  418.6 6.6 collective-permute-start.10
  422.1 5.3 collective-permute-start.11
  579.2 8.0 %copy-start.12 = (f32[128]{0:T(128)}, f32[128]{0:T(128)S(1)}, u32[]{:S(2)}) copy-start(f32[128]{0:T(128)S(1)} %div.26) | copy-start | bytes 1540
  579.4 7.8 %collective-permute-start.13 = (f32[256,128]{0,1:T(8,128)S(1)}, f32[256,128]{0,1:T(8,128)S(1)}, u32[]{:S(2)}, u32[]{:S(2)}) collective-permute-start(f32[256,128]{0,1:T(8,128)S(1)} %get-tuple-element.42), channel_id=1, source_target_pairs={{0,1},{1,2},{2,3},{3,4},{4,5},{5,6},{6,7},{7,8},{8,9},{9,10},{10,1... | collective-permute-start | bytes 393224 | tf_op jit(solution)/shard_map/ppermute | solution.py:21
  579.8 7.4 %collective-permute-start.12 = (f32[256,128]{0,1:T(8,128)S(1)}, f32[256,128]{0,1:T(8,128)S(1)}, u32[]{:S(2)}, u32[]{:S(2)}) collective-permute-start(f32[256,128]{0,1:T(8,128)S(1)} %get-tuple-element.41), channel_id=1, source_target_pairs={{0,32},{32,64},{64,96},{96,128},{128,160},{160,192},{192,224},{1,3... | collective-permute-start | bytes 393224 | tf_op jit(solution)/shard_map/ppermute | solution.py:15
  599.7 9.0 %copy-start.4 = (f32[1,1,1,256,128]{3,4,2,1,0:T(8,128)S(1)}, f32[1,1,1,256,128]{3,4,2,1,0:T(8,128)}, u32[]{:S(2)}) copy-start(f32[1,1,1,256,128]{3,4,2,1,0:T(8,128)} %copy-done.3) | copy-start | bytes 393220
  604.4 86.8 %copy-start.17 = (f32[128]{0:T(128)S(1)}, f32[128]{0:T(128)}, u32[]{:S(2)}) copy-start(f32[128]{0:T(128)} %copy-done.16) | copy-start | bytes 1540
  604.4 86.8 %copy-start.6 = (f32[1,1,1,256,128]{3,4,2,1,0:T(8,128)S(1)}, f32[1,1,1,256,128]{3,4,2,1,0:T(8,128)}, u32[]{:S(2)}) copy-start(f32[1,1,1,256,128]{3,4,2,1,0:T(8,128)} %get-tuple-element.25) | copy-start | bytes 393220
  604.4 86.8 %copy-start.7 = (f32[1,1,1,256,128]{3,4,2,1,0:T(8,128)S(1)}, f32[1,1,1,256,128]{3,4,2,1,0:T(8,128)}, u32[]{:S(2)}) copy-start(f32[1,1,1,256,128]{3,4,2,1,0:T(8,128)} %get-tuple-element.27) | copy-start | bytes 393220
  604.4 86.8 %copy-start.8 = (f32[1,1,1,256,128]{3,4,2,1,0:T(8,128)S(1)}, f32[1,1,1,256,128]{3,4,2,1,0:T(8,128)}, u32[]{:S(2)}) copy-start(f32[1,1,1,256,128]{3,4,2,1,0:T(8,128)} %get-tuple-element.16) | copy-start | bytes 393220
  604.4 86.8 %copy-start.9 = (f32[1,1,1,256,128]{3,4,2,1,0:T(8,128)S(1)}, f32[1,1,1,256,128]{3,4,2,1,0:T(8,128)}, u32[]{:S(2)}) copy-start(f32[1,1,1,256,128]{3,4,2,1,0:T(8,128)} %get-tuple-element.31) | copy-start | bytes 393220
  604.4 86.8 %copy-start.10 = (f32[1,1,1,256,128]{3,4,2,1,0:T(8,128)S(1)}, f32[1,1,1,256,128]{3,4,2,1,0:T(8,128)}, u32[]{:S(2)}) copy-start(f32[1,1,1,256,128]{3,4,2,1,0:T(8,128)} %get-tuple-element.20) | copy-start | bytes 393220
  604.4 86.8 %copy-start.11 = (f32[1,1,1,256,128]{3,4,2,1,0:T(8,128)S(1)}, f32[1,1,1,256,128]{3,4,2,1,0:T(8,128)}, u32[]{:S(2)}) copy-start(f32[1,1,1,256,128]{3,4,2,1,0:T(8,128)} %get-tuple-element.33) | copy-start | bytes 393220
  604.4 86.8 %copy-start.13 = (f32[128]{0:T(128)S(1)}, f32[128]{0:T(128)}, u32[]{:S(2)}) copy-start(f32[128]{0:T(128)} %copy-done.12) | copy-start | bytes 1540
  604.4 86.8 %copy-start.15 = (f32[128]{0:T(128)S(1)}, f32[128]{0:T(128)}, u32[]{:S(2)}) copy-start(f32[128]{0:T(128)} %copy-done.14) | copy-start | bytes 1540
  604.5 6.8 collective-permute-start.14
  608.1 5.3 collective-permute-start.15
  (2 other events, 1.9 us)
where the time goes:
time: 703 us; the launch traced here: 694 us
  blocking collectives  529 us (75%)
  matrix products  61.1 us (9%)
  starting transfers between devices  36.9 us (5%)
  waiting for transfers between devices  34 us (5%)
  local copies, waits for them, and re-layouts  17.6 us (3%)
  other arithmetic  13.2 us (2%)
    psum x4, blocking collectives, norm_of(): return lax.psum(owned_inner(vector, vector), ('floor', 'facade'))  296 us
    psum x3, blocking collectives, local(): lax.psum(owned_inner(direction, image), ('floor', 'facade'))  233 us
    dot_general x4, matrix products, local(): jnp.dot(factor, apply_flat, precision=finest, preferred_element_type=jnp....  28.4 us
    ppermute x8, starting transfers between devices, shifted(): lax.ppermute(value, axis, [(source, source + steps) for source in range(f...  24.6 us
    ppermute x8, waiting for transfers between devices, from_behind(): return lax.ppermute(value, axis, pairs)  22.1 us
    dot_general x4, matrix products, local(): jnp.einsum('ji,jr->ir', factor, inner, precision=finest, preferred_elemen...  18.8 us
  transfers between devices with their start and end apart: 16, of which 11 were waited for; matrix products, arithmetic and copies ran while one was open for 2% of the time, Pallas kernels for 0%

commit v1 on v0

v1 whole, which is shorter than its diff:
```python
import functools

import jax
import jax.numpy as jnp
from jax import lax
from jax.experimental import pallas as pl
from jax.experimental.pallas import tpu as pltpu
from jax.sharding import PartitionSpec as P

ITERS = 4
RING = 4
F32 = jnp.float32
BF16 = jnp.bfloat16


def halves(value):
    high = value.astype(BF16)
    low = (value - high.astype(F32)).astype(BF16)
    return high, low


def kernel(
    floors,
    facades,
    rhs_hbm,
    w_hbm,
    near_hbm,
    pattern,
    x_ref,
    r_ref,
    w_land,
    near_land,
    w_hi,
    w_lo,
    wt_hi,
    wt_lo,
    near,
    near_t,
    a_hi,
    a_lo,
    uu,
    yy,
    recv,
    ww,
    zz,
    pp,
    ss,
    sums_out,
    sums_y,
    sums_f,
    sums_z,
    load_sem,
    face_send,
    face_recv,
    sum_send,
    sum_recv,
):
    size = w_land.shape[0]
    face = size // 4
    blocks = pattern.shape[2]
    blk = size // blocks
    f = lax.axis_index("floor")
    c = lax.axis_index("facade")
    ring = RING
    stack = facades // ring
    ypos = lax.rem(c, ring)
    zpos = lax.div(c, ring)
    keep = {0: (f > 0).astype(F32), 1: (f < floors - 1).astype(F32)}

    up = (lax.rem(f + 1, floors), c)
    down = (lax.rem(f + floors - 1, floors), c)
    right = (f, lax.rem(c + 1, facades))
    left = (f, lax.rem(c + facades - 1, facades))
    y_peers = [(f, zpos * ring + lax.rem(ypos + d, ring)) for d in range(1, ring)]
    f_peers = [(lax.rem(f + d, floors), c) for d in range(1, floors)]
    z_peers = [(f, lax.rem(zpos + d, stack) * ring + ypos) for d in range(1, stack)]

    chunk = size // blocks
    loads = []
    for i in range(blocks):
        rows = pl.ds(i * chunk, chunk)
        loads.append(pltpu.make_async_copy(w_hbm.at[0, 0, rows], w_land.at[rows], load_sem.at[i]))
    near_load = pltpu.make_async_copy(near_hbm.at[0, 0], near_land, load_sem.at[blocks])
    rhs_load = pltpu.make_async_copy(rhs_hbm.at[0, 0], r_ref, load_sem.at[blocks + 1])
    rhs_load.start()
    for copy in loads:
        copy.start()
    near_load.start()

    barrier = pltpu.get_barrier_semaphore()
    greeted = y_peers + f_peers + z_peers + [left, right]
    for peer in greeted:
        pl.semaphore_signal(barrier, inc=1, device_id=peer, device_id_type=pl.DeviceIdType.MESH)
    pl.semaphore_wait(barrier, len(greeted))

    def face_copy(source, k, slot, peer):
        return pltpu.make_async_remote_copy(
            src_ref=source,
            dst_ref=recv.at[k, slot],
            send_sem=face_send.at[k, slot],
            recv_sem=face_recv.at[k, slot],
            device_id=peer,
            device_id_type=pl.DeviceIdType.MESH,
        )

    first = {
        2: face_copy(rhs_hbm.at[0, 0, 1], ITERS, 2, right),
        0: face_copy(rhs_hbm.at[0, 0, 0], ITERS, 0, up),
    }
    for slot in (2, 0):
        first[slot].start()

    def split_rows(i):
        rows = pl.ds(pl.multiple_of(i * chunk, chunk), chunk)
        high, low = halves(w_land[rows, :])
        w_hi[rows, :] = high
        w_lo[rows, :] = low
        wt_hi[:, rows] = high.T
        wt_lo[:, rows] = low.T

    for i in range(blocks):
        loads[i].wait()
        split_rows(i)
    near_load.wait()

    def mask_rows(i, _):
        rows = pl.ds(pl.multiple_of(i * blk, blk), blk)
        for j in range(blocks):
            columns = pl.ds(j * blk, blk)
            kept = near_land[rows, columns].astype(F32) * pattern[0, 0, i, j].astype(F32)
            kept = kept.astype(BF16)
            near[rows, columns] = kept
            near_t[columns, rows] = kept.T
        return 0

    lax.fori_loop(0, blocks, mask_rows, 0)

    def product(left_side, right_side):
        return jnp.dot(left_side, right_side, preferred_element_type=F32)

    for i in range(4):
        rows = pl.ds(i * face, face)
        for j in range(i, 4):
            columns = pl.ds(j * face, face)
            total = product(wt_hi[rows, :], w_hi[:, columns])
            total += product(wt_hi[rows, :], w_lo[:, columns])
            total += product(wt_lo[rows, :], w_hi[:, columns])
            total += product(near_t[rows, :], near[:, columns])
            high, low = halves(total)
            a_hi[rows, columns] = high
            a_lo[rows, columns] = low
            if j > i:
                a_hi[columns, rows] = high.T
                a_lo[columns, rows] = low.T

    def set_input(slot, value):
        rows = pl.ds(slot * face, face)
        ww[rows, :] = value
        high, low = halves(value)
        uu[rows, 0 : value.shape[1]] = high
        uu[rows, value.shape[1] :] = low

    rhs_load.wait()
    r_ref[0] = r_ref[0] * keep[1]
    set_input(1, r_ref[0])
    set_input(3, r_ref[1])
    for slot in (0, 2):
        first[slot].wait()
        got = -recv[ITERS, slot]
        set_input(slot, got * keep[0] if slot == 0 else got)
    x_ref[...] = jnp.zeros_like(x_ref)
    pp[...] = jnp.zeros_like(pp)
    ss[...] = jnp.zeros_like(ss)
    zz[...] = jnp.zeros_like(zz)

    def sum_copy(k, stage, target, mine, peer):
        return pltpu.make_async_remote_copy(
            src_ref=sums_out.at[k, stage],
            dst_ref=target.at[k, mine],
            send_sem=sum_send.at[k, stage],
            recv_sem=sum_recv.at[k, stage],
            device_id=peer,
            device_id_type=pl.DeviceIdType.MESH,
        )

    stages = [(sums_y, ypos, y_peers), (sums_f, f, f_peers), (sums_z, zpos, z_peers)]

    def sums_start(k, stage, value):
        target, mine, peers = stages[stage]
        sums_out[k, stage] = value
        target[k, mine] = value
        for peer in peers:
            sum_copy(k, stage, target, mine, peer).start()

    def sums_end(k, stage):
        target, mine, peers = stages[stage]
        arrived = target.at[k, pl.ds(0, len(peers))]
        pltpu.make_async_copy(arrived, arrived, sum_recv.at[k, stage]).wait()
        total = target[k, 0]
        for i in range(1, len(peers) + 1):
            total += target[k, i]
        return total

    def own_sums():
        gamma = jnp.zeros((1, x_ref.shape[2]), F32)
        delta = gamma
        for own, slot in ((0, 1), (1, 3)):
            value = r_ref[own]
            gamma += jnp.sum(value * value, axis=0, keepdims=True)
            delta += jnp.sum(value * ww[slot * face : (slot + 1) * face, :], axis=0, keepdims=True)
        return jnp.concatenate([gamma, delta, jnp.zeros((6, gamma.shape[1]), F32)], axis=0)

    def apply_rows(k, slot):
        rows = pl.ds(slot * face, face)
        wide = product(a_hi[rows, :], uu[...]) + product(a_lo[rows, :], uu[...])
        cases = x_ref.shape[2]
        yy[k, slot] = wide[:, :cases] + wide[:, cases:]

    def coefficients(total, last_gamma, last_alpha):
        gamma = total[0:1]
        delta = total[1:2]
        beta = gamma / last_gamma
        alpha = gamma / (delta - beta * gamma / last_alpha)
        return gamma, alpha, beta

    def step_own(own, alpha, beta, old_w):
        fresh_s = old_w + beta * ss[own]
        fresh_p = r_ref[own] + beta * pp[own]
        ss[own] = fresh_s
        pp[own] = fresh_p
        x_ref[own] = x_ref[own] + alpha * fresh_p
        r_ref[own] = r_ref[own] - alpha * fresh_s

    def iteration(k, carry):
        last_gamma, last_alpha = carry
        first_time = k == 0
        begin = jnp.where(first_time, 1.0, 0.0).astype(F32)
        sums_start(k, 0, own_sums())
        apply_rows(k, 2)
        face_copy(yy.at[k, 2], k, 3, left).start()
        apply_rows(k, 3)
        face_copy(yy.at[k, 3], k, 2, right).start()
        sums_start(k, 1, sums_end(k, 0))
        apply_rows(k, 0)
        face_copy(yy.at[k, 0], k, 1, down).start()
        apply_rows(k, 1)
        face_copy(yy.at[k, 1], k, 0, up).start()
        sums_start(k, 2, sums_end(k, 1))
        total = sums_end(k, 2)
        gamma, alpha, beta = coefficients(total, last_gamma, last_alpha)
        alpha_w = alpha * (1.0 - begin) - begin
        alpha_x = alpha * (1.0 - begin)
        for slot in (0, 1, 2, 3):
            rows = pl.ds(slot * face, face)
            pltpu.make_async_copy(recv.at[k, slot], recv.at[k, slot], face_recv.at[k, slot]).wait()
            image = yy[k, slot] - recv[k, slot]
            if slot in keep:
                image = image * keep[slot]
            fresh_z = image + beta * zz[rows, :]
            zz[rows, :] = fresh_z
            old_w = ww[rows, :]
            if slot % 2 == 1:
                step_own(slot // 2, alpha_x, beta, old_w)
            set_input(slot, (1.0 - begin) * old_w - alpha_w * fresh_z)
        next_gamma = jnp.where(first_time, jnp.full_like(gamma, jnp.inf), gamma)
        next_alpha = jnp.where(first_time, jnp.ones_like(alpha), alpha)
        return next_gamma, next_alpha

    ones = jnp.ones((1, x_ref.shape[2]), F32)
    carry = (ones * jnp.inf, ones)
    carry = lax.fori_loop(0, ITERS, iteration, carry)

    sums_start(ITERS, 0, own_sums())
    sums_start(ITERS, 1, sums_end(ITERS, 0))
    sums_start(ITERS, 2, sums_end(ITERS, 1))
    total = sums_end(ITERS, 2)
    gamma, alpha, beta = coefficients(total, *carry)
    for own, slot in ((0, 1), (1, 3)):
        step_own(own, alpha, beta, ww[slot * face : (slot + 1) * face, :])

    def drain(k, _):
        for slot in range(4):
            pltpu.make_async_copy(recv.at[k, slot], recv.at[k, slot], face_send.at[k, slot]).wait()
        return 0

    lax.fori_loop(0, ITERS, drain, 0)

    def drain_sums(k, _):
        for stage in range(3):
            target, mine, peers = stages[stage]
            sent = target.at[k, pl.ds(0, len(peers))]
            pltpu.make_async_copy(sent, sent, sum_send.at[k, stage]).wait()
        return 0

    lax.fori_loop(0, ITERS + 1, drain_sums, 0)


def solution(mesh):
    floors = mesh.shape["floor"]
    facades = mesh.shape["facade"]

    def local(interface_rhs, inverse_factor, near_coupling, near_pattern):
        face, cases = interface_rhs.shape[3:]
        size = 4 * face
        blocks = near_pattern.shape[2]
        own = (2, face, cases)
        square = (size, size)
        outs = pl.pallas_call(
            functools.partial(kernel, floors, facades),
            out_shape=(jax.ShapeDtypeStruct(own, F32), jax.ShapeDtypeStruct(own, F32)),
            in_specs=[
                pl.BlockSpec(memory_space=pl.ANY),
                pl.BlockSpec(memory_space=pl.ANY),
                pl.BlockSpec(memory_space=pl.ANY),
                pl.BlockSpec(memory_space=pltpu.SMEM),
            ],
            out_specs=(
                pl.BlockSpec(memory_space=pltpu.VMEM),
                pl.BlockSpec(memory_space=pltpu.VMEM),
            ),
            scratch_shapes=[
                pltpu.VMEM(square, F32),
                pltpu.VMEM(square, BF16),
                pltpu.VMEM(square, BF16),
                pltpu.VMEM(square, BF16),
                pltpu.VMEM(square, BF16),
                pltpu.VMEM(square, BF16),
                pltpu.VMEM(square, BF16),
                pltpu.VMEM(square, BF16),
                pltpu.VMEM(square, BF16),
                pltpu.VMEM(square, BF16),
                pltpu.VMEM((size, 2 * cases), BF16),
                pltpu.VMEM((ITERS, 4, face, cases), F32),
                pltpu.VMEM((ITERS + 1, 4, face, cases), F32),
                pltpu.VMEM((size, cases), F32),
                pltpu.VMEM((size, cases), F32),
                pltpu.VMEM(own, F32),
                pltpu.VMEM(own, F32),
                pltpu.VMEM((ITERS + 1, 3, 8, cases), F32),
                pltpu.VMEM((ITERS + 1, RING, 8, cases), F32),
                pltpu.VMEM((ITERS + 1, floors, 8, cases), F32),
                pltpu.VMEM((ITERS + 1, facades // RING, 8, cases), F32),
                pltpu.SemaphoreType.DMA((blocks + 2,)),
                pltpu.SemaphoreType.DMA((ITERS + 1, 4)),
                pltpu.SemaphoreType.DMA((ITERS + 1, 4)),
                pltpu.SemaphoreType.DMA((ITERS + 1, 3)),
                pltpu.SemaphoreType.DMA((ITERS + 1, 3)),
            ],
            compiler_params=pltpu.CompilerParams(
                collective_id=0, has_side_effects=True, vmem_limit_bytes=48 << 20
            ),
        )(interface_rhs, inverse_factor, near_coupling, near_pattern)
        return tuple(value[None, None] for value in outs)

    vector = P("floor", "facade", None, None, None)
    matrix = P("floor", "facade", None, None)
    return jax.shard_map(
        local,
        mesh=mesh,
        in_specs=(vector, matrix, matrix, matrix),
        out_specs=(vector, vector),
        check_vma=False,
    )
```

time: 703 us -> 85.5 us (0.12); the launches traced: 694 us -> 85.3 us
  blocking collectives: 529 us -> 0 us
  Pallas kernels: 0 us -> 80 us
  matrix products: 61.1 us -> 0 us
  starting transfers between devices: 36.9 us -> 0 us
  waiting for transfers between devices: 34 us -> 0 us
  other arithmetic: 13.2 us -> 0 us
  local copies, waits for them, and re-layouts: 17.6 us -> 4.63 us
    psum x7 -> x0, blocking collectives: 529 us -> none  [the longest x4 296 us: norm_of(): return lax.psum(owned_inner(vector, vector), ('floor', 'facade'))]
    pallas_call x0 -> x1, Pallas kernels: none -> 80 us  [local(): pl.pallas_call(functools.partial(kernel, floors, facades), out_shape=(jax...]
    dot_general x12 -> x0, matrix products: 61.1 us -> none  [the longest x4 28.4 us: local(): jnp.dot(factor, apply_flat, precision=finest, preferred_element_type=jnp....]
    ppermute x16 -> x0, starting transfers between devices: 36.9 us -> none  [the longest x8 24.6 us: shifted(): lax.ppermute(value, axis, [(source, source + steps) for source in range(f...]
    ppermute x16 -> x0, waiting for transfers between devices: 34 us -> none  [the longest x8 22.1 us: from_behind(): return lax.ppermute(value, axis, pairs)]
  transfers between devices with their start and end apart: 16 -> 0, of which waited for: 11 -> 0; matrix products, arithmetic and copies ran while one was open for 2% -> 0% of each run, Pallas kernels for 0% -> 0%
where the time goes in v1:
time: 85.5 us; the launch traced here: 85.3 us
  Pallas kernels  80 us (94%)
  local copies, waits for them, and re-layouts  4.63 us (5%)
    pallas_call x1, Pallas kernels, local(): pl.pallas_call(functools.partial(kernel, floors, facades), out_shape=(jax...  80 us
    unnamed x8, local copies, waits for them, and re-layouts  4.63 us

profile of v1, /device:TPU:1, one launch (start us, length us, event | category | flops | bytes accessed | tf_op | source)
XLA Modules:
  0.0 85.3 jit_solution(2498083714464231948)
XLA Ops:
  0.6 0.0 copy-start
  0.6 1.6 %copy-done = bf16[1,1,1024,1024]{3,2,1,0:T(8,128)(2,1)S(1)} copy-done((bf16[1,1,1024,1024]{3,2,1,0:T(8,128)(2,1)S(1)}, bf16[1,1,1024,1024]{3,2,1,0:T(8,128)(2,1)}, u32[]{:S(2)}) %copy-start) | copy-done | bytes 2097176
  2.2 0.0 copy-start.1
  2.2 0.9 %copy-done.1 = f32[1,1,2,256,128]{4,3,2,1,0:T(8,128)S(1)} copy-done((f32[1,1,2,256,128]{4,3,2,1,0:T(8,128)S(1)}, f32[1,1,2,256,128]{4,3,2,1,0:T(8,128)}, u32[]{:S(2)}) %copy-start.1) | copy-done | bytes 262168
  3.2 0.0 copy-start.2
  3.2 0.7 copy-done.2
  3.9 80.0 %shard_map.59 = (f32[2,256,128]{2,1,0:T(8,128)S(1)}, f32[2,256,128]{2,1,0:T(8,128)S(1)}) custom-call(f32[1,1,2,256,128]{4,3,2,1,0:T(8,128)S(1)} %copy-done.1, f32[1,1,1024,1024]{3,2,1,0:T(8,128)} %w_hbm.1, bf16[1,1,1024,1024]{3,2,1,0:T(8,128)(2,1)S(1)} %copy-done, s32[1,1,8,8]{3,2,1,0:T(8,128)S(1)} %copy-done.2), custom_call_target="tpu_custom_call" | custom-call | tf_op jit(solution)/shard_map/pallas_call | solution.py:308
  83.9 0.7 copy.8
  84.6 0.7 copy.9
Async XLA Ops:
  0.6 1.6 %copy-start = (bf16[1,1,1024,1024]{3,2,1,0:T(8,128)(2,1)S(1)}, bf16[1,1,1024,1024]{3,2,1,0:T(8,128)(2,1)}, u32[]{:S(2)}) copy-start(bf16[1,1,1024,1024]{3,2,1,0:T(8,128)(2,1)} %near_hbm.1) | copy-start | bytes 6291460
  2.2 0.9 %copy-start.1 = (f32[1,1,2,256,128]{4,3,2,1,0:T(8,128)S(1)}, f32[1,1,2,256,128]{4,3,2,1,0:T(8,128)}, u32[]{:S(2)}) copy-start(f32[1,1,2,256,128]{4,3,2,1,0:T(8,128)} %rhs_hbm.1) | copy-start | bytes 786436
  3.2 0.7 copy-start.2

commit v2 on v1

v2 whole, which is shorter than its diff:
```python
import functools

import jax
import jax.numpy as jnp
from jax import lax
from jax.experimental import pallas as pl
from jax.experimental.pallas import tpu as pltpu
from jax.sharding import PartitionSpec as P

ITERS = 4
RING = 4
F32 = jnp.float32
BF16 = jnp.bfloat16
MESH = pl.DeviceIdType.MESH


def halves(value):
    high = value.astype(BF16)
    low = (value - high.astype(F32)).astype(BF16)
    return high, low


def product(left_side, right_side):
    return jnp.dot(left_side, right_side, preferred_element_type=F32)


def tile_sum(value):
    rows, columns = value.shape
    tall = jnp.sum(value.reshape(rows // 8, 8, columns), axis=0)
    total = tall[:, 0:128]
    for start in range(128, columns, 128):
        total += tall[:, start : start + 128]
    return total


def column_sum(left_side, right_side):
    return jnp.sum(left_side * right_side, axis=0, keepdims=True)


def hankel_solve(entries, given):
    count = len(given)
    lower = [[None] * count for _ in range(count)]
    pivots = []
    for j in range(count):
        pivot = entries[2 * j]
        for k in range(j):
            pivot = pivot - lower[j][k] * lower[j][k] * pivots[k]
        pivots.append(pivot)
        for i in range(j + 1, count):
            value = entries[i + j]
            for k in range(j):
                value = value - lower[i][k] * lower[j][k] * pivots[k]
            lower[i][j] = value / pivot
    middle = []
    for i in range(count):
        value = given[i]
        for k in range(i):
            value = value - lower[i][k] * middle[k]
        middle.append(value)
    answer = [None] * count
    for i in reversed(range(count)):
        value = middle[i] / pivots[i]
        for k in range(i + 1, count):
            value = value - lower[k][i] * answer[k]
        answer[i] = value
    return answer


def kernel(
    floors,
    facades,
    rhs_hbm,
    w_hbm,
    near_hbm,
    pattern,
    x_ref,
    r_ref,
    w_land,
    near_land,
    rhs_land,
    w_hi,
    w_lo,
    wt_hi,
    wt_lo,
    near,
    near_t,
    a_ref,
    uu,
    part,
    yy,
    recv,
    vv,
    sums_out,
    sums_plane,
    sums_z,
    load_sem,
    face_send,
    face_recv,
    sum_send,
    sum_recv,
):
    size = w_land.shape[0]
    face = size // 4
    cases = x_ref.shape[2]
    blocks = pattern.shape[2]
    blk = size // blocks
    half = 2 * face
    f = lax.axis_index("floor")
    c = lax.axis_index("facade")
    stack = facades // RING
    ypos = lax.rem(c, RING)
    zpos = lax.div(c, RING)
    keep = {0: (f > 0).astype(F32), 1: (f < floors - 1).astype(F32)}

    up = (lax.rem(f + 1, floors), c)
    down = (lax.rem(f + floors - 1, floors), c)
    right = (f, lax.rem(c + 1, facades))
    left = (f, lax.rem(c + facades - 1, facades))
    steps = [(i, j) for i in range(floors) for j in range(RING) if i or j]
    steps.sort(key=lambda s: -(min(s[0], floors - s[0]) / 2 + min(s[1], RING - s[1])))
    plane_peers = [
        (lax.rem(f + i, floors), zpos * RING + lax.rem(ypos + j, RING)) for i, j in steps
    ]
    far = sorted(range(1, stack), key=lambda d: -min(d, stack - d))
    z_peers = [(f, lax.rem(zpos + d, stack) * RING + ypos) for d in far]

    loads = []
    for i in range(blocks):
        rows = pl.ds(i * blk, blk)
        loads.append(pltpu.make_async_copy(w_hbm.at[0, 0, rows], w_land.at[rows], load_sem.at[i]))
    near_load = pltpu.make_async_copy(near_hbm.at[0, 0], near_land, load_sem.at[blocks])
    rhs_load = pltpu.make_async_copy(rhs_hbm.at[0, 0], rhs_land, load_sem.at[blocks + 1])
    rhs_load.start()
    for copy in loads:
        copy.start()
    near_load.start()

    barrier = pltpu.get_barrier_semaphore()
    greeted = plane_peers + z_peers + [left, right]
    for peer in greeted:
        pl.semaphore_signal(barrier, inc=1, device_id=peer, device_id_type=MESH)

    squares = jnp.zeros((8, 128), F32)
    for i in range(blocks):
        loads[i].wait()
        rows = pl.ds(i * blk, blk)
        value = w_land[rows, :]
        high, low = halves(value)
        w_hi[rows, :] = high
        w_lo[rows, :] = low
        wt_hi[:, rows] = high.T
        wt_lo[:, rows] = low.T
        squares += tile_sum(value * value)

    rhs_load.wait()
    pl.semaphore_wait(barrier, len(greeted))

    def face_copy(source, k, slot, peer):
        return pltpu.make_async_remote_copy(
            src_ref=source,
            dst_ref=recv.at[k, slot],
            send_sem=face_send.at[k, slot],
            recv_sem=face_recv.at[k, slot],
            device_id=peer,
            device_id_type=MESH,
        )

    first = {
        2: face_copy(rhs_land.at[1], ITERS, 2, right),
        0: face_copy(rhs_land.at[0], ITERS, 0, up),
    }
    for slot in (2, 0):
        first[slot].start()

    near_load.wait()

    def mask_rows(i, total):
        rows = pl.ds(pl.multiple_of(i * blk, blk), blk)
        for j in range(blocks):
            columns = pl.ds(j * blk, blk)
            kept = near_land[rows, columns].astype(F32) * pattern[0, 0, i, j].astype(F32)
            total += tile_sum(kept * kept)
            kept = kept.astype(BF16)
            near[rows, columns] = kept
            near_t[columns, rows] = kept.T
        return total

    squares = lax.fori_loop(0, blocks, mask_rows, squares)

    stages = [
        (sums_plane, f * RING + ypos, plane_peers),
        (sums_z, zpos, z_peers),
    ]

    def sums_start(turn, stage, value):
        target, mine, peers = stages[stage]
        sums_out[turn, stage] = value
        target[turn, mine] = value
        for peer in peers:
            pltpu.make_async_remote_copy(
                src_ref=sums_out.at[turn, stage],
                dst_ref=target.at[turn, mine],
                send_sem=sum_send.at[turn, stage],
                recv_sem=sum_recv.at[turn, stage],
                device_id=peer,
                device_id_type=MESH,
            ).start()

    def sums_end(turn, stage):
        target, _, peers = stages[stage]
        arrived = target.at[turn, pl.ds(0, len(peers))]
        pltpu.make_async_copy(arrived, arrived, sum_recv.at[turn, stage]).wait()
        terms = [target[turn, i] for i in range(len(peers) + 1)]
        while len(terms) > 1:
            terms = [a + b for a, b in zip(terms[0::2], terms[1::2])]
        return terms[0]

    sums_start(0, 0, squares)

    for i in range(4):
        rows = pl.ds(i * face, face)
        for j in range(i, 4):
            columns = pl.ds(j * face, face)
            total = product(wt_hi[rows, :], w_hi[:, columns])
            total += product(wt_hi[rows, :], w_lo[:, columns])
            total += product(wt_lo[rows, :], w_hi[:, columns])
            total += product(near_t[rows, :], near[:, columns])
            high, low = halves(total)
            a_ref[i, 0, :, columns] = high
            a_ref[i, 1, :, columns] = low
            if j > i:
                a_ref[j, 0, :, rows] = high.T
                a_ref[j, 1, :, rows] = low.T

    def set_input(k, slot, value):
        vv[k, slot] = value
        rows = pl.ds(slot * face, face)
        high, low = halves(value)
        uu[rows, 0:cases] = high
        uu[rows, cases : 2 * cases] = low

    def products_of(slots, columns):
        slot = slots[0]
        lines = a_ref[slot : slot + 2, :, :, columns].reshape(4 * face, half)
        wide = product(lines, uu[columns, :])
        wide = wide[:, 0:cases] + wide[:, cases : 2 * cases]
        wide = wide.reshape(2, 2, face, cases)
        return [wide[i, 0] + wide[i, 1] for i in range(2)]

    def first_half():
        for slots in ((2, 3), (0, 1)):
            for slot, value in zip(slots, products_of(slots, pl.ds(0, half))):
                part[slot] = value

    def second_half(k, slots):
        for slot, value in zip(slots, products_of(slots, pl.ds(half, half))):
            yy[k, slot] = part[slot] + value

    def own_sums(left_side, right_side):
        return column_sum(vv[left_side, 1], vv[right_side, 1]) + column_sum(
            vv[left_side, 3], vv[right_side, 3]
        )

    def image_of(k, slot):
        image = yy[k, slot] - recv[k, slot]
        return image * keep[slot] if slot in keep else image

    set_input(0, 1, rhs_land[0] * keep[1])
    set_input(0, 3, rhs_land[1])
    first[0].wait()
    set_input(0, 0, -recv[ITERS, 0] * keep[0])
    first_half()
    sums_start(0, 1, sums_end(0, 0))
    first[2].wait()
    set_input(0, 2, -recv[ITERS, 2])

    moments = []
    sends = {0: (1, down), 1: (0, up), 2: (3, left), 3: (2, right)}
    for k in range(ITERS - 1):
        for slots in ((2, 3), (0, 1)):
            second_half(k, slots)
            for slot in slots:
                target, peer = sends[slot]
                face_copy(yy.at[k, slot], k, target, peer).start()
        if k > 0:
            moments.append(own_sums(k - 1, k))
        moments.append(own_sums(k, k))
        if k == 0:
            total = sums_end(0, 1)
            count = float(floors * facades * size)
            shift = jnp.sum(jnp.sum(total, axis=0, keepdims=True), axis=1, keepdims=True)
            shift = jnp.broadcast_to(shift * (2.0 / count), (1, cases))
            scale = 1.0 / shift
        for slot in (0, 1, 2, 3):
            pltpu.make_async_copy(recv.at[k, slot], recv.at[k, slot], face_recv.at[k, slot]).wait()
            fresh = (image_of(k, slot) - shift * vv[k, slot]) * scale
            set_input(k + 1, slot, fresh)
            if slot == 1:
                first_half()

    last = ITERS - 1
    second_half(last, (2, 3))
    second_half(last, (0, 1))
    energy = column_sum(vv[last, 0], yy[last, 0])
    for slot in range(1, 4):
        energy += column_sum(vv[last, slot], yy[last, slot])
    moments.append(own_sums(last - 1, last))
    moments.append(own_sums(last, last))
    sums_start(1, 0, jnp.concatenate(moments + [energy], axis=0))
    for slot in (2, 0):
        target, peer = sends[slot]
        face_copy(yy.at[last, slot], last, target, peer).start()
    sums_start(1, 1, sums_end(1, 0))
    total = sums_end(1, 1)

    given = [total[i : i + 1] for i in range(2 * ITERS - 1)]
    entries = [given[i + 1] * shift + given[i] * shift for i in range(2 * ITERS - 2)]
    entries.append(total[2 * ITERS - 1 : 2 * ITERS])
    answer = hankel_solve(entries, given[:ITERS])
    weights = []
    for i in range(ITERS):
        weight = (1.0 if i == 0 else -answer[i - 1] * shift) - answer[i] * shift if i < last else (
            -answer[i - 1] * shift
        )
        weights.append(weight)
    for own, slot in ((1, 3), (0, 1)):
        pltpu.make_async_copy(
            recv.at[last, slot], recv.at[last, slot], face_recv.at[last, slot]
        ).wait()
        solved = answer[0] * vv[0, slot]
        left_over = weights[0] * vv[0, slot]
        for i in range(1, ITERS):
            solved += answer[i] * vv[i, slot]
            left_over += weights[i] * vv[i, slot]
        x_ref[own] = solved
        r_ref[own] = left_over - answer[last] * image_of(last, slot)

    for k in range(ITERS):
        for slot in sends if k < last else (1, 3):
            pltpu.make_async_copy(recv.at[k, slot], recv.at[k, slot], face_send.at[k, slot]).wait()
    for turn in range(2):
        for stage in range(2):
            target, _, peers = stages[stage]
            sent = target.at[turn, pl.ds(0, len(peers))]
            pltpu.make_async_copy(sent, sent, sum_send.at[turn, stage]).wait()


def solution(mesh):
    floors = mesh.shape["floor"]
    facades = mesh.shape["facade"]

    def local(interface_rhs, inverse_factor, near_coupling, near_pattern):
        face, cases = interface_rhs.shape[3:]
        size = 4 * face
        blocks = near_pattern.shape[2]
        own = (2, face, cases)
        square = (size, size)
        outs = pl.pallas_call(
            functools.partial(kernel, floors, facades),
            out_shape=(jax.ShapeDtypeStruct(own, F32), jax.ShapeDtypeStruct(own, F32)),
            in_specs=[
                pl.BlockSpec(memory_space=pltpu.HBM),
                pl.BlockSpec(memory_space=pltpu.HBM),
                pl.BlockSpec(memory_space=pltpu.HBM),
                pl.BlockSpec(memory_space=pltpu.SMEM),
            ],
            out_specs=(
                pl.BlockSpec(memory_space=pltpu.VMEM),
                pl.BlockSpec(memory_space=pltpu.VMEM),
            ),
            scratch_shapes=[
                pltpu.VMEM(square, F32),
                pltpu.VMEM(square, BF16),
                pltpu.VMEM(own, F32),
                pltpu.VMEM(square, BF16),
                pltpu.VMEM(square, BF16),
                pltpu.VMEM(square, BF16),
                pltpu.VMEM(square, BF16),
                pltpu.VMEM(square, BF16),
                pltpu.VMEM(square, BF16),
                pltpu.VMEM((4, 2, face, size), BF16),
                pltpu.VMEM((size, 2 * cases), BF16),
                pltpu.VMEM((4, face, cases), F32),
                pltpu.VMEM((ITERS, 4, face, cases), F32),
                pltpu.VMEM((ITERS + 1, 4, face, cases), F32),
                pltpu.VMEM((ITERS, 4, face, cases), F32),
                pltpu.VMEM((2, 2, 8, cases), F32),
                pltpu.VMEM((2, floors * RING, 8, cases), F32),
                pltpu.VMEM((2, facades // RING, 8, cases), F32),
                pltpu.SemaphoreType.DMA((blocks + 2,)),
                pltpu.SemaphoreType.DMA((ITERS + 1, 4)),
                pltpu.SemaphoreType.DMA((ITERS + 1, 4)),
                pltpu.SemaphoreType.DMA((2, 2)),
                pltpu.SemaphoreType.DMA((2, 2)),
            ],
            compiler_params=pltpu.CompilerParams(
                collective_id=0, has_side_effects=True, vmem_limit_bytes=60 << 20
            ),
        )(interface_rhs, inverse_factor, near_coupling, near_pattern)
        return tuple(value[None, None] for value in outs)

    vector = P("floor", "facade", None, None, None)
    matrix = P("floor", "facade", None, None)
    return jax.shard_map(
        local,
        mesh=mesh,
        in_specs=(vector, matrix, matrix, matrix),
        out_specs=(vector, vector),
        check_vma=False,
    )
```

time: 85.5 us -> 54.7 us (0.64)
  Pallas kernels: 80 us -> 50.6 us
  local copies, waits for them, and re-layouts: 4.63 us -> 3.34 us
    pallas_call x1, Pallas kernels: 80 us -> 50.6 us  [local(): pl.pallas_call(functools.partial(kernel, floors, facades), out_shape=(jax...]
    unnamed x8 -> x2, local copies, waits for them, and re-layouts: 4.63 us -> 3.34 us
where the time goes in v2:
time: 54.7 us; the launch traced here: 54.6 us
  Pallas kernels  50.6 us (93%)
  local copies, waits for them, and re-layouts  3.34 us (6%)
  between operations  0.64 us (1%)
    pallas_call x1, Pallas kernels, local(): pl.pallas_call(functools.partial(kernel, floors, facades), out_shape=(jax...  50.6 us
    unnamed x2, local copies, waits for them, and re-layouts  3.34 us

profile of v2, /device:TPU:1, one launch (start us, length us, event | category | flops | bytes accessed | tf_op | source)
XLA Modules:
  0.0 54.6 jit_solution(4941422455848951051)
XLA Ops:
  0.6 50.6 %shard_map.59 = (f32[2,256,128]{2,1,0:T(8,128)}, f32[2,256,128]{2,1,0:T(8,128)}) custom-call(f32[1,1,2,256,128]{4,3,2,1,0:T(8,128)} %rhs_hbm.1, f32[1,1,1024,1024]{3,2,1,0:T(8,128)} %w_hbm.1, bf16[1,1,1024,1024]{3,2,1,0:T(8,128)(2,1)} %near_hbm.1, s32[1,1,8,8]{3,2,1,0:T(8,128)} %pattern.1), custom_call_target="tpu_custom_call" | custom-call | tf_op jit(solution)/shard_map/pallas_call | solution.py:358
  51.2 1.7 %copy.8 = f32[1,1,2,256,128]{4,3,2,1,0:T(8,128)} copy(f32[1,1,2,256,128]{4,3,2,1,0:T(8,128)} %bitcast.3) | data formatting | bytes 524288
  52.9 1.7 %copy.9 = f32[1,1,2,256,128]{4,3,2,1,0:T(8,128)} copy(f32[1,1,2,256,128]{4,3,2,1,0:T(8,128)} %bitcast.2) | data formatting | bytes 524288

commit v3 on v2

--- a/solution.py
+++ b/solution.py
@@ -72,12 +72,13 @@
     rhs_hbm,
     w_hbm,
     near_hbm,
-    pattern,
+    pattern_hbm,
     x_ref,
     r_ref,
     w_land,
     near_land,
     rhs_land,
+    pattern,
     w_hi,
     w_lo,
     wt_hi,
@@ -93,6 +94,9 @@
     sums_out,
     sums_plane,
     sums_z,
+    few_out,
+    few_plane,
+    few_z,
     load_sem,
     face_send,
     face_recv,
@@ -102,7 +106,7 @@
     size = w_land.shape[0]
     face = size // 4
     cases = x_ref.shape[2]
-    blocks = pattern.shape[2]
+    blocks = pattern.shape[0]
     blk = size // blocks
     half = 2 * face
     f = lax.axis_index("floor")
@@ -130,10 +134,12 @@
         loads.append(pltpu.make_async_copy(w_hbm.at[0, 0, rows], w_land.at[rows], load_sem.at[i]))
     near_load = pltpu.make_async_copy(near_hbm.at[0, 0], near_land, load_sem.at[blocks])
     rhs_load = pltpu.make_async_copy(rhs_hbm.at[0, 0], rhs_land, load_sem.at[blocks + 1])
+    pattern_load = pltpu.make_async_copy(pattern_hbm.at[0, 0], pattern, load_sem.at[blocks + 2])
     rhs_load.start()
     for copy in loads:
         copy.start()
     near_load.start()
+    pattern_load.start()
 
     barrier = pltpu.get_barrier_semaphore()
     greeted = plane_peers + z_peers + [left, right]
@@ -173,12 +179,13 @@
         first[slot].start()
 
     near_load.wait()
+    pattern_load.wait()
 
     def mask_rows(i, total):
         rows = pl.ds(pl.multiple_of(i * blk, blk), blk)
         for j in range(blocks):
             columns = pl.ds(j * blk, blk)
-            kept = near_land[rows, columns].astype(F32) * pattern[0, 0, i, j].astype(F32)
+            kept = near_land[rows, columns].astype(F32) * pattern[i, j].astype(F32)
             total += tile_sum(kept * kept)
             kept = kept.astype(BF16)
             near[rows, columns] = kept
@@ -187,30 +194,37 @@
 
     squares = lax.fori_loop(0, blocks, mask_rows, squares)
 
-    stages = [
-        (sums_plane, f * RING + ypos, plane_peers),
-        (sums_z, zpos, z_peers),
-    ]
+    mine = (f * RING + ypos, zpos)
+    peers_of = (plane_peers, z_peers)
+
+    def buffers(turn, stage):
+        if turn == 2:
+            return few_out.at[stage], (few_plane, few_z)[stage]
+        return sums_out.at[turn, stage], (sums_plane, sums_z)[stage].at[turn]
 
     def sums_start(turn, stage, value):
-        target, mine, peers = stages[stage]
-        sums_out[turn, stage] = value
-        target[turn, mine] = value
-        for peer in peers:
+        source, target = buffers(turn, stage)
+        source[...] = value
+        target[mine[stage]] = value
+        for peer in peers_of[stage]:
             pltpu.make_async_remote_copy(
-                src_ref=sums_out.at[turn, stage],
-                dst_ref=target.at[turn, mine],
+                src_ref=source,
+                dst_ref=target.at[mine[stage]],
                 send_sem=sum_send.at[turn, stage],
                 recv_sem=sum_recv.at[turn, stage],
                 device_id=peer,
                 device_id_type=MESH,
             ).start()
 
+    def sums_wait(turn, stage, semaphores):
+        _, target = buffers(turn, stage)
+        moved = target.at[pl.ds(0, len(peers_of[stage]))]
+        pltpu.make_async_copy(moved, moved, semaphores.at[turn, stage]).wait()
+
     def sums_end(turn, stage):
-        target, _, peers = stages[stage]
-        arrived = target.at[turn, pl.ds(0, len(peers))]
-        pltpu.make_async_copy(arrived, arrived, sum_recv.at[turn, stage]).wait()
-        terms = [target[turn, i] for i in range(len(peers) + 1)]
+        sums_wait(turn, stage, sum_recv)
+        _, target = buffers(turn, stage)
+        terms = [target[i] for i in range(len(peers_of[stage]) + 1)]
         while len(terms) > 1:
             terms = [a + b for a, b in zip(terms[0::2], terms[1::2])]
         return terms[0]
@@ -274,9 +288,10 @@
     first[2].wait()
     set_input(0, 2, -recv[ITERS, 2])
 
+    last = ITERS - 1
     moments = []
     sends = {0: (1, down), 1: (0, up), 2: (3, left), 3: (2, right)}
-    for k in range(ITERS - 1):
+    for k in range(last):
         for slots in ((2, 3), (0, 1)):
             second_half(k, slots)
             for slot in slots:
@@ -285,6 +300,9 @@
         if k > 0:
             moments.append(own_sums(k - 1, k))
         moments.append(own_sums(k, k))
+        if k == last - 1:
+            blank = [jnp.zeros_like(moments[0])] * (8 - len(moments))
+            sums_start(1, 0, jnp.concatenate(moments + blank, axis=0))
         if k == 0:
             total = sums_end(0, 1)
             count = float(floors * facades * size)
@@ -298,24 +316,24 @@
             if slot == 1:
                 first_half()
 
-    last = ITERS - 1
     second_half(last, (2, 3))
     second_half(last, (0, 1))
     energy = column_sum(vv[last, 0], yy[last, 0])
     for slot in range(1, 4):
         energy += column_sum(vv[last, slot], yy[last, slot])
-    moments.append(own_sums(last - 1, last))
-    moments.append(own_sums(last, last))
-    sums_start(1, 0, jnp.concatenate(moments + [energy], axis=0))
+    late = [own_sums(last - 1, last), own_sums(last, last), energy, jnp.zeros_like(energy)]
+    sums_start(2, 0, jnp.concatenate(late, axis=0))
     for slot in (2, 0):
         target, peer = sends[slot]
         face_copy(yy.at[last, slot], last, target, peer).start()
     sums_start(1, 1, sums_end(1, 0))
-    total = sums_end(1, 1)
-
-    given = [total[i : i + 1] for i in range(2 * ITERS - 1)]
+    sums_start(2, 1, sums_end(2, 0))
+    early = sums_end(1, 1)
+    final = sums_end(2, 1)
+
+    given = [early[i : i + 1] for i in range(len(moments))] + [final[0:1], final[1:2]]
     entries = [given[i + 1] * shift + given[i] * shift for i in range(2 * ITERS - 2)]
-    entries.append(total[2 * ITERS - 1 : 2 * ITERS])
+    entries.append(final[2:3])
     answer = hankel_solve(entries, given[:ITERS])
     weights = []
     for i in range(ITERS):
@@ -338,18 +356,17 @@
     for k in range(ITERS):
         for slot in sends if k < last else (1, 3):
             pltpu.make_async_copy(recv.at[k, slot], recv.at[k, slot], face_send.at[k, slot]).wait()
-    for turn in range(2):
+    for turn in range(3):
         for stage in range(2):
-            target, _, peers = stages[stage]
-            sent = target.at[turn, pl.ds(0, len(peers))]
-            pltpu.make_async_copy(sent, sent, sum_send.at[turn, stage]).wait()
+            sums_wait(turn, stage, sum_send)
 
 
 def solution(mesh):
     floors = mesh.shape["floor"]
     facades = mesh.shape["facade"]
 
-    def local(interface_rhs, inverse_factor, near_coupling, near_pattern):
+    def local(*operands):
+        interface_rhs, _, _, near_pattern = operands
         face, cases = interface_rhs.shape[3:]
         size = 4 * face
         blocks = near_pattern.shape[2]
@@ -362,7 +379,7 @@
                 pl.BlockSpec(memory_space=pltpu.HBM),
                 pl.BlockSpec(memory_space=pltpu.HBM),
                 pl.BlockSpec(memory_space=pltpu.HBM),
-                pl.BlockSpec(memory_space=pltpu.SMEM),
+                pl.BlockSpec(memory_space=pltpu.HBM),
             ],
             out_specs=(
                 pl.BlockSpec(memory_space=pltpu.VMEM),
@@ -372,6 +389,7 @@
                 pltpu.VMEM(square, F32),
                 pltpu.VMEM(square, BF16),
                 pltpu.VMEM(own, F32),
+                pltpu.SMEM((blocks, blocks), jnp.int32),
                 pltpu.VMEM(square, BF16),
                 pltpu.VMEM(square, BF16),
                 pltpu.VMEM(square, BF16),
@@ -387,16 +405,19 @@
                 pltpu.VMEM((2, 2, 8, cases), F32),
                 pltpu.VMEM((2, floors * RING, 8, cases), F32),
                 pltpu.VMEM((2, facades // RING, 8, cases), F32),
-                pltpu.SemaphoreType.DMA((blocks + 2,)),
+                pltpu.VMEM((2, 4, cases), F32),
+                pltpu.VMEM((floors * RING, 4, cases), F32),
+                pltpu.VMEM((facades // RING, 4, cases), F32),
+                pltpu.SemaphoreType.DMA((blocks + 3,)),
                 pltpu.SemaphoreType.DMA((ITERS + 1, 4)),
                 pltpu.SemaphoreType.DMA((ITERS + 1, 4)),
-                pltpu.SemaphoreType.DMA((2, 2)),
-                pltpu.SemaphoreType.DMA((2, 2)),
+                pltpu.SemaphoreType.DMA((3, 2)),
+                pltpu.SemaphoreType.DMA((3, 2)),
             ],
             compiler_params=pltpu.CompilerParams(
-                collective_id=0, has_side_effects=True, vmem_limit_bytes=60 << 20
+                collective_id=0, has_side_effects=True, vmem_limit_bytes=48 << 20
             ),
-        )(interface_rhs, inverse_factor, near_coupling, near_pattern)
+        )(*(pltpu.with_memory_space_constraint(value, pltpu.HBM) for value in operands))
         return tuple(value[None, None] for value in outs)
 
     vector = P("floor", "facade", None, None, None)

time: 54.7 us -> 52.1 us (0.952)
  local copies, waits for them, and re-layouts: 3.34 us -> 1.41 us
  Pallas kernels: 50.6 us -> 49.9 us
    unnamed x2, local copies, waits for them, and re-layouts: 3.34 us -> 1.41 us
    pallas_call x1, Pallas kernels: 50.6 us -> 49.9 us  [local(): pl.pallas_call(functools.partial(kernel, floors, facades), out_shape=(jax...]
where the time goes in v3:
time: 52.1 us; the launch traced here: 52 us
  Pallas kernels  49.9 us (96%)
  local copies, waits for them, and re-layouts  1.41 us (3%)
  between operations  0.64 us (1%)
    pallas_call x1, Pallas kernels, local(): pl.pallas_call(functools.partial(kernel, floors, facades), out_shape=(jax...  49.9 us
    unnamed x2, local copies, waits for them, and re-layouts  1.41 us

profile of v3, /device:TPU:1, one launch (start us, length us, event | category | flops | bytes accessed | tf_op | source)
XLA Modules:
  0.0 52.0 jit_solution(2556859158939713380)
XLA Ops:
  0.6 49.9 %shard_map.59 = (f32[2,256,128]{2,1,0:T(8,128)S(1)}, f32[2,256,128]{2,1,0:T(8,128)S(1)}) custom-call(f32[1,1,2,256,128]{4,3,2,1,0:T(8,128)} %rhs_hbm.1, f32[1,1,1024,1024]{3,2,1,0:T(8,128)} %w_hbm.1, bf16[1,1,1024,1024]{3,2,1,0:T(8,128)(2,1)} %near_hbm.1, s32[1,1,8,8]{3,2,1,0:T(8,128)} %pattern_hbm.1), custom_call_target="tpu_custom_call" | custom-call | tf_op jit(solution)/shard_map/pallas_call | solution.py:375
  50.6 0.7 %copy.8 = f32[1,1,2,256,128]{4,3,2,1,0:T(8,128)} copy(f32[1,1,2,256,128]{4,3,2,1,0:T(8,128)S(1)} %bitcast.3) | data formatting | bytes 524288
  51.3 0.7 %copy.9 = f32[1,1,2,256,128]{4,3,2,1,0:T(8,128)} copy(f32[1,1,2,256,128]{4,3,2,1,0:T(8,128)S(1)} %bitcast.2) | data formatting | bytes 524288

commit v4 on v3

--- a/solution.py
+++ b/solution.py
@@ -198,9 +198,9 @@
     peers_of = (plane_peers, z_peers)
 
     def buffers(turn, stage):
-        if turn == 2:
-            return few_out.at[stage], (few_plane, few_z)[stage]
-        return sums_out.at[turn, stage], (sums_plane, sums_z)[stage].at[turn]
+        if turn == 1:
+            return sums_out.at[stage], (sums_plane, sums_z)[stage]
+        return few_out.at[turn // 2, stage], (few_plane, few_z)[stage].at[turn // 2]
 
     def sums_start(turn, stage, value):
         source, target = buffers(turn, stage)
@@ -229,7 +229,7 @@
             terms = [a + b for a, b in zip(terms[0::2], terms[1::2])]
         return terms[0]
 
-    sums_start(0, 0, squares)
+    sums_start(0, 0, squares[0:4] + squares[4:8])
 
     for i in range(4):
         rows = pl.ds(i * face, face)
@@ -361,6 +361,17 @@
             sums_wait(turn, stage, sum_send)
 
 
+def write_out(x_ref, r_ref, x_out, r_out, sems):
+    copies = [
+        pltpu.make_async_copy(x_ref, x_out.at[0, 0], sems.at[0]),
+        pltpu.make_async_copy(r_ref, r_out.at[0, 0], sems.at[1]),
+    ]
+    for copy in copies:
+        copy.start()
+    for copy in copies:
+        copy.wait()
+
+
 def solution(mesh):
     floors = mesh.shape["floor"]
     facades = mesh.shape["facade"]
@@ -402,12 +413,12 @@
                 pltpu.VMEM((ITERS, 4, face, cases), F32),
                 pltpu.VMEM((ITERS + 1, 4, face, cases), F32),
                 pltpu.VMEM((ITERS, 4, face, cases), F32),
-                pltpu.VMEM((2, 2, 8, cases), F32),
-                pltpu.VMEM((2, floors * RING, 8, cases), F32),
-                pltpu.VMEM((2, facades // RING, 8, cases), F32),
-                pltpu.VMEM((2, 4, cases), F32),
-                pltpu.VMEM((floors * RING, 4, cases), F32),
-                pltpu.VMEM((facades // RING, 4, cases), F32),
+                pltpu.VMEM((2, 8, cases), F32),
+                pltpu.VMEM((floors * RING, 8, cases), F32),
+                pltpu.VMEM((facades // RING, 8, cases), F32),
+                pltpu.VMEM((2, 2, 4, cases), F32),
+                pltpu.VMEM((2, floors * RING, 4, cases), F32),
+                pltpu.VMEM((2, facades // RING, 4, cases), F32),
                 pltpu.SemaphoreType.DMA((blocks + 3,)),
                 pltpu.SemaphoreType.DMA((ITERS + 1, 4)),
                 pltpu.SemaphoreType.DMA((ITERS + 1, 4)),
@@ -418,7 +429,15 @@
                 collective_id=0, has_side_effects=True, vmem_limit_bytes=48 << 20
             ),
         )(*(pltpu.with_memory_space_constraint(value, pltpu.HBM) for value in operands))
-        return tuple(value[None, None] for value in outs)
+        whole = jax.ShapeDtypeStruct((1, 1, *own), F32)
+        return pl.pallas_call(
+            write_out,
+            out_shape=(whole, whole),
+            in_specs=[pl.BlockSpec(memory_space=pltpu.VMEM)] * 2,
+            out_specs=[pl.BlockSpec(memory_space=pltpu.HBM)] * 2,
+            scratch_shapes=[pltpu.SemaphoreType.DMA((2,))],
+            compiler_params=pltpu.CompilerParams(vmem_limit_bytes=1 << 20),
+        )(*(pltpu.with_memory_space_constraint(value, pltpu.VMEM) for value in outs))
 
     vector = P("floor", "facade", None, None, None)
     matrix = P("floor", "facade", None, None)

time: 52.1 us -> 51.3 us (0.985)
  local copies, waits for them, and re-layouts: 1.41 us -> 0 us
  Pallas kernels: 49.9 us -> 50.6 us
    unnamed x2 -> x0, local copies, waits for them, and re-layouts: 1.41 us -> none
    pallas_call x0 -> x1, Pallas kernels: none -> 0.81 us  [local(): pl.pallas_call(write_out, out_shape=(whole, whole), in_specs=[pl.BlockSpe...]
where the time goes in v4:
time: 51.3 us
  Pallas kernels  50.6 us (99%)
  between operations  0.64 us (1%)
    pallas_call x1, Pallas kernels, local(): pl.pallas_call(functools.partial(kernel, floors, facades), out_shape=(jax...  49.8 us

profile of v4, /device:TPU:1, one launch (start us, length us, event | category | flops | bytes accessed | tf_op | source)
XLA Modules:
  0.0 51.3 jit_solution(1180921293550094206)
XLA Ops:
  0.6 49.8 %shard_map.59 = (f32[2,256,128]{2,1,0:T(8,128)S(1)}, f32[2,256,128]{2,1,0:T(8,128)S(1)}) custom-call(f32[1,1,2,256,128]{4,3,2,1,0:T(8,128)} %rhs_hbm.1, f32[1,1,1024,1024]{3,2,1,0:T(8,128)} %w_hbm.1, bf16[1,1,1024,1024]{3,2,1,0:T(8,128)(2,1)} %near_hbm.1, s32[1,1,8,8]{3,2,1,0:T(8,128)} %pattern_hbm.1), custom_call_target="tpu_custom_call" | custom-call | tf_op jit(solution)/shard_map/pallas_call | solution.py:386
  50.5 0.8 %shard_map.60 = (f32[1,1,2,256,128]{4,3,2,1,0:T(8,128)}, f32[1,1,2,256,128]{4,3,2,1,0:T(8,128)}) custom-call(f32[2,256,128]{2,1,0:T(8,128)S(1)} %get-tuple-element.4.x_ref, f32[2,256,128]{2,1,0:T(8,128)S(1)} %get-tuple-element.5.r_ref), custom_call_target="tpu_custom_call" | custom-call | tf_op jit(solution)/shard_map/pallas_call | solution.py:433

commit v5 on v4

--- a/solution.py
+++ b/solution.py
@@ -317,12 +317,12 @@
                 first_half()
 
     second_half(last, (2, 3))
-    second_half(last, (0, 1))
-    energy = column_sum(vv[last, 0], yy[last, 0])
-    for slot in range(1, 4):
-        energy += column_sum(vv[last, slot], yy[last, slot])
+    energy = column_sum(vv[last, 0], part[0]) + column_sum(vv[last, 1], part[1])
+    for slot in (2, 3):
+        energy += column_sum(vv[last, slot], part[slot] + yy[last, slot])
     late = [own_sums(last - 1, last), own_sums(last, last), energy, jnp.zeros_like(energy)]
     sums_start(2, 0, jnp.concatenate(late, axis=0))
+    second_half(last, (0, 1))
     for slot in (2, 0):
         target, peer = sends[slot]
         face_copy(yy.at[last, slot], last, target, peer).start()

time: 51.3 us -> 51.3 us (level)
  no operation moved by 1% of the time
where the time goes in v5:
time: 51.3 us; the launch traced here: 51.2 us
  Pallas kernels  50.6 us (99%)
  between operations  0.64 us (1%)
    pallas_call x1, Pallas kernels, local(): pl.pallas_call(functools.partial(kernel, floors, facades), out_shape=(jax...  49.8 us

profile of v5, /device:TPU:1, one launch (start us, length us, event | category | flops | bytes accessed | tf_op | source)
XLA Modules:
  0.0 51.2 jit_solution(16167260232324905682)
XLA Ops:
  0.6 49.8 %shard_map.59 = (f32[2,256,128]{2,1,0:T(8,128)S(1)}, f32[2,256,128]{2,1,0:T(8,128)S(1)}) custom-call(f32[1,1,2,256,128]{4,3,2,1,0:T(8,128)} %rhs_hbm.1, f32[1,1,1024,1024]{3,2,1,0:T(8,128)} %w_hbm.1, bf16[1,1,1024,1024]{3,2,1,0:T(8,128)(2,1)} %near_hbm.1, s32[1,1,8,8]{3,2,1,0:T(8,128)} %pattern_hbm.1), custom_call_target="tpu_custom_call" | custom-call | tf_op jit(solution)/shard_map/pallas_call | solution.py:386
  50.4 0.8 %shard_map.60 = (f32[1,1,2,256,128]{4,3,2,1,0:T(8,128)}, f32[1,1,2,256,128]{4,3,2,1,0:T(8,128)}) custom-call(f32[2,256,128]{2,1,0:T(8,128)S(1)} %get-tuple-element.4.x_ref, f32[2,256,128]{2,1,0:T(8,128)S(1)} %get-tuple-element.5.r_ref), custom_call_target="tpu_custom_call" | custom-call | tf_op jit(solution)/shard_map/pallas_call | solution.py:433
